TPU v7x, 256 devices: a whole 4x4x8 slice. The times are simulated.
256 devices in a mesh: dp: 4 (over y_hi, core), seq: 8 (over z), head: 8 (over x, y_lo).
Axes of the slice: x: 4, y: 4 (y_hi: 2, y_lo: 2; y = y_hi * 2 + y_lo), z: 8, core: 2. Of those that a mesh axis runs over, the one named last changes fastest.
Arguments:
- tokens: bfloat16 [4, 8192, 512], P('dp', ('seq', 'head')), may hold values from -800 to 800
- bin_ids: int32 [4, 8192], P('dp'), may hold values from 0 to 127, never falling along the last dimension, each value on 1 to 256 neighbouring positions
- pattern: int32 [4, 64, 9], P('dp'), may hold values from 0 to 63, as said below
- w_qkv: bfloat16 [512, 1536], replicated, may hold values from -3.2 to 3.2
- w_out: bfloat16 [512, 512], replicated, may hold values from -5 to 5
- head_bias: float32 [8], replicated, may hold values from -3 to 400
- grad_output: bfloat16 [4, 8192, 512], P('dp', ('seq', 'head')), may hold values from -6 to 6
Outputs:
- output: bfloat16 [4, 8192, 512], P('dp', ('seq', 'head'))
- grad_tokens: bfloat16 [4, 8192, 512], P('dp', ('seq', 'head'))
- grad_w_qkv: float32 [512, 1536], P(None, 'head')
- grad_w_out: float32 [512, 512], P('head')
Inputs may be any that keep to these rules, and one draw needn't show every extreme that they name: `pattern`: row i of sequence b lists (i + o) mod 64 for the 9 offsets o of sequence b, in the same order in every row: 0, 1, -1, then distinct a from 2 to 31, then their negatives. So block J is in row I exactly when I is in row J. `bin_ids`: bin numbers never fall along a sequence.
All inputs are finite; a program needn't handle non-finite values.
Results may differ from a plain program's by a relative error of at most 0.01.
Values may be sent and summed in bfloat16 or wider, within the bound.
A program may use at most 64 MiB of HBM per device.

v0:
```python
import math
import jax
import jax.numpy as jnp
from jax import lax
from jax.sharding import PartitionSpec as P

D = 512
HEADS = 8
HD = 64
BLK = 128
NNZ = 9
EPSILON = 1e-05


def normalize(token_rows):
    widened = token_rows.astype(jnp.float32)
    spread = jnp.sqrt(jnp.mean(widened * widened, axis=-1, keepdims=True) + EPSILON)
    return (widened / spread, spread)


def query_scores(query_blk, key_blk, bin_query, bin_key, bias_local, factor):
    raw_scores = jnp.einsum(
        "gqhe,gnkhe->ghqnk", query_blk, key_blk, preferred_element_type=jnp.float32
    )
    same_bin = (bin_query[:, None, :, None, None] == bin_key[:, None, None, :, :]).astype(
        jnp.float32
    )
    scores = raw_scores * factor + bias_local[None, :, None, None, None] * same_bin
    return scores.reshape(scores.shape[0], scores.shape[1], scores.shape[2], -1)


def body(tokens, bin_ids, pattern, w_qkv, w_out, head_bias, grad_output):
    tok_rows = tokens.shape[1]
    head_parts = lax.axis_size("head")
    local_heads = HEADS // head_parts
    seq_rows = tok_rows * head_parts
    seq_length = bin_ids.shape[1]
    blocks_all = seq_length // BLK
    local_blocks = seq_rows // BLK
    group_size = math.gcd(local_blocks, 4)
    group_count = local_blocks // group_size
    factor = 1.0 / math.sqrt(HD)
    seq_pos = lax.axis_index("seq")
    head_pos = lax.axis_index("head")
    first_block = seq_pos * local_blocks
    key_lists = lax.dynamic_slice_in_dim(pattern[0], first_block, local_blocks, 0)
    bin_table = bin_ids[0].reshape(blocks_all, BLK)
    bin_local = lax.dynamic_slice_in_dim(bin_table, first_block, local_blocks, 0)
    bias_local = lax.dynamic_slice_in_dim(head_bias, head_pos * local_heads, local_heads, 0)

    def grouped(array):
        return array.reshape((group_count, group_size) + array.shape[1:])

    normed, spread = normalize(tokens[0])
    hidden = normed.astype(jnp.bfloat16)
    packed = jnp.dot(hidden, w_qkv, preferred_element_type=jnp.float32).astype(jnp.bfloat16)
    packed = packed.reshape(tok_rows, HEADS, 3 * HD)
    packed_heads = lax.all_to_all(packed, "head", split_axis=1, concat_axis=0, tiled=True)
    queries = packed_heads[:, :, :HD]
    pair_local = packed_heads[:, :, HD:]
    pair_all = lax.all_gather(pair_local, "seq", axis=0, tiled=True)
    pair_table = pair_all.reshape(blocks_all, BLK, local_heads, 2 * HD)
    query_blocks = queries.reshape(local_blocks, BLK, local_heads, HD)

    def forward_group(entries):
        query_blk, key_rows, bin_query = entries
        pair_blk = jnp.take(pair_table, key_rows, axis=0)
        bin_key = jnp.take(bin_table, key_rows, axis=0)
        scores = query_scores(query_blk, pair_blk[..., :HD], bin_query, bin_key, bias_local, factor)
        row_max = jnp.max(scores, axis=-1, keepdims=True)
        log_total = row_max + jnp.log(jnp.sum(jnp.exp(scores - row_max), axis=-1, keepdims=True))
        probs = jnp.exp(scores - log_total).astype(jnp.bfloat16)
        value_flat = pair_blk[..., HD:].reshape(group_size, NNZ * BLK, local_heads, HD)
        attended = jnp.einsum(
            "ghqm,gmhe->gqhe", probs, value_flat, preferred_element_type=jnp.float32
        )
        return (attended.astype(jnp.bfloat16), log_total[..., 0])

    attended, log_blocks = lax.map(
        forward_group, (grouped(query_blocks), grouped(key_lists), grouped(bin_local))
    )
    attended_heads = attended.reshape(seq_rows, local_heads, HD)
    log_blocks = log_blocks.reshape(local_blocks, local_heads, BLK)
    attended_tok = lax.all_to_all(
        attended_heads, "head", split_axis=0, concat_axis=1, tiled=True
    ).reshape(tok_rows, D)
    result = jnp.dot(attended_tok, w_out, preferred_element_type=jnp.float32).astype(jnp.bfloat16)
    grad_rows = grad_output[0]
    grad_att = jnp.dot(grad_rows, w_out.T, preferred_element_type=jnp.float32).astype(jnp.bfloat16)
    grad_heads = lax.all_to_all(
        grad_att.reshape(tok_rows, HEADS, HD), "head", split_axis=1, concat_axis=0, tiled=True
    )
    delta_rows = jnp.sum(
        grad_heads.astype(jnp.float32) * attended_heads.astype(jnp.float32), axis=-1
    )
    delta_blocks = delta_rows.reshape(local_blocks, BLK, local_heads).swapaxes(1, 2)
    grad_blocks = grad_heads.reshape(local_blocks, BLK, local_heads, HD)

    def query_core(entries):
        query_blk, grad_blk, log_blk, delta_blk, key_rows, bin_query = entries
        pair_blk = jnp.take(pair_table, key_rows, axis=0)
        bin_key = jnp.take(bin_table, key_rows, axis=0)
        scores = query_scores(query_blk, pair_blk[..., :HD], bin_query, bin_key, bias_local, factor)
        probs = jnp.exp(scores - log_blk[..., None])
        value_flat = pair_blk[..., HD:].reshape(group_size, NNZ * BLK, local_heads, HD)
        key_flat = pair_blk[..., :HD].reshape(group_size, NNZ * BLK, local_heads, HD)
        grad_prob = jnp.einsum(
            "gqhe,gmhe->ghqm", grad_blk, value_flat, preferred_element_type=jnp.float32
        )
        grad_score = (probs * (grad_prob - delta_blk[..., None]) * factor).astype(jnp.bfloat16)
        grad_query = jnp.einsum(
            "ghqm,gmhe->gqhe", grad_score, key_flat, preferred_element_type=jnp.float32
        )
        return (grad_query.astype(jnp.bfloat16), grad_score, probs)

    query_entries = (
        grouped(query_blocks),
        grouped(grad_blocks),
        grouped(log_blocks),
        grouped(delta_blocks),
        grouped(key_lists),
        grouped(bin_local),
    )

    def scatter_step(carried, entries):
        query_blk, grad_blk = (entries[0], entries[1])
        key_rows = entries[4]
        grad_query, grad_score, probs = query_core(entries)
        key_part = jnp.einsum(
            "ghqm,gqhe->gmhe", grad_score, query_blk, preferred_element_type=jnp.float32
        )
        value_part = jnp.einsum(
            "ghqm,gqhe->gmhe",
            probs.astype(jnp.bfloat16),
            grad_blk,
            preferred_element_type=jnp.float32,
        )
        both_parts = jnp.concatenate([key_part, value_part], axis=-1)
        both_parts = both_parts.reshape(group_size * NNZ, BLK, local_heads, 2 * HD)
        carried = carried.at[key_rows.reshape(-1)].add(both_parts)
        return (carried, grad_query)

    empty_sum = jnp.zeros((blocks_all, BLK, local_heads, 2 * HD), jnp.float32)
    pair_sums, grad_queries = lax.scan(scatter_step, empty_sum, query_entries)
    own_pairs = lax.psum_scatter(
        pair_sums.reshape(seq_length, local_heads, 2 * HD), "seq", scatter_dimension=0, tiled=True
    )
    grad_pairs = own_pairs.astype(jnp.bfloat16)
    grad_packed_heads = jnp.concatenate(
        [grad_queries.reshape(seq_rows, local_heads, HD), grad_pairs], axis=-1
    )
    grad_packed = lax.all_to_all(
        grad_packed_heads, "head", split_axis=0, concat_axis=1, tiled=True
    ).reshape(tok_rows, 3 * D)
    grad_hidden = jnp.dot(grad_packed, w_qkv.T, preferred_element_type=jnp.float32)
    inner = jnp.mean(grad_hidden * normed, axis=-1, keepdims=True)
    grad_input = ((grad_hidden - normed * inner) / spread).astype(jnp.bfloat16)
    local_qkv = jnp.einsum("td,tc->dc", hidden, grad_packed, preferred_element_type=jnp.float32)
    local_out = jnp.einsum("td,tc->dc", grad_rows, attended_tok, preferred_element_type=jnp.float32)
    total_qkv, total_out = lax.psum((local_qkv, local_out), ("dp", "seq", "head"))
    own_qkv = lax.dynamic_slice_in_dim(
        total_qkv, head_pos * local_heads * 3 * HD, local_heads * 3 * HD, 1
    )
    own_out = lax.dynamic_slice_in_dim(total_out, head_pos * local_heads * HD, local_heads * HD, 1)
    return (result[None], grad_input[None], own_qkv, own_out.T)


def solution(mesh):
    return jax.shard_map(
        body,
        mesh=mesh,
        in_specs=(
            P("dp", ("seq", "head"), None),
            P("dp", None),
            P("dp", None, None),
            P(),
            P(),
            P(),
            P("dp", ("seq", "head"), None),
        ),
        out_specs=(
            P("dp", ("seq", "head"), None),
            P("dp", ("seq", "head"), None),
            P(None, "head"),
            P("head", None),
        ),
        check_vma=False,
    )
```

profile of v0, /device:TPU:2, one launch (start us, length us, event | category | flops | bytes accessed | tf_op | source)
XLA Modules:
  0.0 558.7 jit_solution(6286347255980764140)
XLA Ops:
  10.6 12.6 %all_to_all.63 = bf16[128,8,192]{0,2,1:T(8,128)(2,1)S(1)} all-to-all(bf16[128,8,192]{0,2,1:T(8,128)(2,1)S(1)} %bitcast.271), channel_id=1, replica_groups=mesh['dp'=4,'seq'=8,'head'=8] {'head'}, dimensions={1} | all-to-all | bytes 786432 | tf_op jit(solution)/shard_map/all_to_all | solution.py:58
  25.1 4.8 all-to-all-start.2
  30.9 36.5 %all-gather.2.cloned.1.call-done = bf16[8192,1,128]{0,2,1:T(8,128)(2,1)} async-done(((bf16[1024,1,128]{0,2,1:T(8,128)(2,1)}), bf16[8192,1,128]{0,2,1:T(8,128)(2,1)}) %all-gather.2.cloned.1.call-update) | async-done | bytes 2097168 | tf_op jit(solution)/shard_map/all_gather | solution.py:61
  67.4 4.1 copy.119
  72.1 40.3 %while.24 = (s32[]{:T(128)}, bf16[2,4,128,1,64]{2,4,1,3,0:T(8,128)(2,1)}, f32[2,4,1,128]{3,1,2,0:T(4,128)}, s32[2,4,9]{2,1,0:T(4,128)S(1)}, bf16[64,128,1,128]{3...) while((s32[]{:T(128)}, ...), condition=%wide.region_4.7_spmd, body=%wide.region_1.6_spmd.sunk | while | flops 156931296 | bytes 39141280 | solution.py:79
  73.5 3.4 gather_fusion
  76.9 1.7 copy.151
  80.7 3.7 fusion.80
  86.2 3.1 copy.153
  89.3 2.3 fusion.81
  93.6 3.4 gather_fusion
  97.0 1.7 copy.151
  100.8 3.7 fusion.80
  106.3 3.1 copy.153
  109.4 2.3 fusion.81
  114.1 2.5 broadcast_in_dim.54
  116.5 86.1 %while.25 = (s32[]{:T(128)}, f32[64,128,1,128]{3,1,0,2:T(8,128)}, bf16[2,4,128,1,64]{2,4,1,3,0:T(8,128)(2,1)}, s32[2,4,9]{2,1,0:T(4,128)S(1)}, bf16[2,4,128,1,64...) while((s32[]{:T(128)}, f32[64,128,1,128]{3,1,0,2:T(8,128)}, ...), condition=%wide.region_8.11_spmd, body=%wide.region_6.10_spmd.sunk | while | flops 385783744 | bytes 64560684 | solution.py:144
  119.2 2.4 gather_fusion.3
  126.9 1.5 reshape.431
  128.3 2.5 copy.158
  130.9 2.1 reshape.432
  133.0 4.2 select_add_fusion.3
  137.2 3.1 copy.155
  140.3 2.5 fusion.94
  144.9 1.6 pad_maximum_fusion.3
  146.5 3.1 copy.157
  149.6 10.0 %scatter_fusion = f32[64,128,128]{2,1,0:T(8,128)} fusion(f32[64,128,128]{2,1,0:T(8,128)} %bitcast.263, s32[36]{0:T(128)S(1)} %copy-done.24, f32[36,128,128]{2,1,0:T(8,128)} %bitcast.257), kind=kCustom, calls=%fused_computation.4.clone.1 | custom fusion | flops 589824 | bytes 7078032 | tf_op jit(solution)/shard_map/while/body/eval_jaxpr/scatter-add | solution.py:140
  162.2 2.4 gather_fusion.3
  169.8 1.5 reshape.431
  171.3 2.5 copy.158
  173.8 2.1 reshape.432
  176.0 4.2 select_add_fusion.3
  180.2 3.1 copy.155
  183.3 2.5 fusion.94
  187.8 1.6 pad_maximum_fusion.3
  189.4 3.1 copy.157
  192.5 10.0 %scatter_fusion = f32[64,128,128]{2,1,0:T(8,128)} fusion(f32[64,128,128]{2,1,0:T(8,128)} %bitcast.263, s32[36]{0:T(128)S(1)} %copy-done.24, f32[36,128,128]{2,1,0:T(8,128)} %bitcast.257), kind=kCustom, calls=%fused_computation.4.clone.1 | custom fusion | flops 589824 | bytes 7078032 | tf_op jit(solution)/shard_map/while/body/eval_jaxpr/scatter-add | solution.py:140
  204.5 2.3 reduce.9
  207.7 5.7 %all-to-all-start.1 = ((bf16[8,2,4096]{2,1,0:T(2,128)(2,1)}), bf16[8,2,4096]{2,1,0:T(2,128)(2,1)S(1)}, u32[]{:S(2)}, u32[]{:S(2)}) async-start(bf16[8,2,4096]{2,1,0:T(2,128)(2,1)} %reshape.393), calls=%async_computation.1 | async-start | bytes 262144 | tf_op jit(solution)/shard_map/all_to_all | solution.py:84
  213.8 43.0 %reduce-scatter.2.cloned.1.call-done = f32[1024,1,128]{2,1,0:T(1,128)} async-done(((f32[8192,1,128]{2,1,0:T(1,128)}), f32[1024,1,128]{2,1,0:T(1,128)}) %reduce-scatter.2.cloned.1.call-update) | async-done | bytes 524304 | tf_op jit(solution)/shard_map/reduce_scatter | solution.py:145
  258.2 2.0 pad_maximum_fusion.1
  260.2 4.1 reduce.10
  265.6 5.7 %all-to-all-start.3 = ((bf16[8,2,12288]{2,1,0:T(2,128)(2,1)}), bf16[8,2,12288]{2,1,0:T(2,128)(2,1)S(1)}, u32[]{:S(2)}, u32[]{:S(2)}) async-start(bf16[8,2,12288]{2,1,0:T(2,128)(2,1)} %reshape.395), calls=%async_computation.4 | async-start | bytes 786432 | tf_op jit(solution)/shard_map/all_to_all | solution.py:152
  273.3 4.7 all-to-all-done.3
  279.5 2.3 fusion.38
  285.3 263.5 %all-reduce.3.cloned.1.call-done = (f32[512,1536]{0,1:T(8,128)}, f32[512,512]{0,1:T(8,128)}) async-done(((f32[512,1536]{0,1:T(8,128)}, f32[512,512]{0,1:T(8,128)}), (f32[512,1536]{0,1:T(8,128)}, f32[512,512]{0,1:T(8,128)})) %all-reduce.3.cloned.1.call-update) | async-done | bytes 4194320 | tf_op jit(solution)/shard_map/psum | solution.py:160
  548.8 1.8 constant_dynamic-slice_fusion.1
  550.6 1.6 dynamic-slice_bitcast_fusion.4
  (200 shorter events, 52.6 us)
Async XLA Ops:
  7.2 1.8 copy-start
  7.2 60.2 %all-gather.2.cloned.1.call-start = ((), (), s32[]{:S(2)}) async-start(), calls=%async_computation.5 | async-start | bytes 2359296 | tf_op jit(solution)/shard_map/all_gather | solution.py:61
  9.0 15.1 %copy-start.6 = (bf16[512,512]{1,0:T(8,128)(2,1)S(1)}, bf16[512,512]{1,0:T(8,128)(2,1)}, u32[]{:S(2)}) copy-start(bf16[512,512]{1,0:T(8,128)(2,1)} %param.19) | copy-start | bytes 1572868
  9.0 15.1 %copy-start.17 = (bf16[1,128,512]{2,1,0:T(8,128)(2,1)S(1)}, bf16[1,128,512]{2,1,0:T(8,128)(2,1)}, u32[]{:S(2)}) copy-start(bf16[1,128,512]{2,1,0:T(8,128)(2,1)} %param.21) | copy-start | bytes 393220
  10.3 19.6 %copy-start.25 = (s32[1,64,9]{1,0,2:T(1,128)S(1)}, s32[1,64,9]{1,0,2:T(1,128)}, u32[]{:S(2)}) copy-start(s32[1,64,9]{1,0,2:T(1,128)} %param.17) | copy-start | bytes 6916
  10.4 19.8 %copy-start.28 = (f32[8]{0:T(128)S(1)}, f32[8]{0:T(128)}, u32[]{:S(2)}) copy-start(f32[8]{0:T(128)} %param.20) | copy-start | bytes 100
  10.4 20.4 %copy-start.3 = (s32[1,8192]{1,0:T(1,128)S(1)}, s32[1,8192]{1,0:T(1,128)}, u32[]{:S(2)}) copy-start(s32[1,8192]{1,0:T(1,128)} %param.16) | copy-start | bytes 98308
  25.1 87.3 %all-to-all-start.2 = ((bf16[128,8,64]{0,2,1:T(8,128)(2,1)}), bf16[128,8,64]{0,2,1:T(8,128)(2,1)S(1)}, u32[]{:S(2)}, u32[]{:S(2)}) async-start(bf16[128,8,64]{0,2,1:T(8,128)(2,1)} %bitcast.50), calls=%async_computation.2 | async-start | bytes 262144 | tf_op jit(solution)/shard_map/all_to_all | solution.py:90
  29.9 226.8 %reduce-scatter.2.cloned.1.call-start = ((), (), s32[]{:S(2)}) async-start(), calls=%async_computation.6 | async-start | bytes 4718592 | tf_op jit(solution)/shard_map/reduce_scatter | solution.py:145
  78.8 1.0 copy-start.4
  79.8 0.8 copy-start.19
  80.7 5.4 copy-start.22
  84.3 1.4 copy-start.2
  86.1 3.2 copy-start.23
  86.1 3.1 copy-start.10
  98.9 1.0 copy-start.4
  100.0 0.8 copy-start.19
  100.8 5.4 copy-start.22
  104.5 1.4 copy-start.2
  106.3 3.2 copy-start.23
  106.3 3.1 copy-start.10
  116.5 2.6 copy-start.20
  116.5 6.5 %copy-start.8 = (bf16[2,4,128,1,64]{2,4,1,3,0:T(8,128)(2,1)}, bf16[2,4,128,1,64]{2,4,1,3,0:T(8,128)(2,1)S(1)}, u32[]{:S(2)}) copy-start(bf16[2,4,128,1,64]{2,4,1,3,0:T(8,128)(2,1)S(1)} %get-tuple-element.496) | copy-start | bytes 393220 | tf_op jit(solution)/shard_map/while
  140.3 2.5 copy-start.1
  142.8 1.1 copy-start.5
  142.9 1.1 copy-start.14
  142.9 1.6 copy-start.9
  144.5 1.9 copy-start.15
  146.5 3.1 copy-start.24
  149.6 10.0 %copy-start.21 = (f32[2,4,1,128]{3,1,2,0:T(4,128)S(1)}, f32[2,4,1,128]{3,1,2,0:T(4,128)}, u32[]{:S(2)}) copy-start(f32[2,4,1,128]{3,1,2,0:T(4,128)} %copy-done.20) | copy-start | bytes 12292 | tf_op jit(solution)/shard_map/while
  159.5 2.6 copy-start.20
  159.5 6.5 %copy-start.8 = (bf16[2,4,128,1,64]{2,4,1,3,0:T(8,128)(2,1)}, bf16[2,4,128,1,64]{2,4,1,3,0:T(8,128)(2,1)S(1)}, u32[]{:S(2)}) copy-start(bf16[2,4,128,1,64]{2,4,1,3,0:T(8,128)(2,1)S(1)} %get-tuple-element.496) | copy-start | bytes 393220 | tf_op jit(solution)/shard_map/while
  183.3 2.5 copy-start.1
  185.8 1.1 copy-start.5
  185.8 1.1 copy-start.14
  185.8 1.6 copy-start.9
  187.5 1.9 copy-start.15
  189.4 3.1 copy-start.24
  192.5 10.0 %copy-start.21 = (f32[2,4,1,128]{3,1,2,0:T(4,128)S(1)}, f32[2,4,1,128]{3,1,2,0:T(4,128)}, u32[]{:S(2)}) copy-start(f32[2,4,1,128]{3,1,2,0:T(4,128)} %copy-done.20) | copy-start | bytes 12292 | tf_op jit(solution)/shard_map/while
  202.6 0.9 copy-start.12
  203.5 9.9 %copy-start.16 = (bf16[2,4,128,1,64]{2,4,1,3,0:T(8,128)(2,1)S(1)}, bf16[2,4,128,1,64]{2,4,1,3,0:T(8,128)(2,1)}, u32[]{:S(2)}) copy-start(bf16[2,4,128,1,64]{2,4,1,3,0:T(8,128)(2,1)} %get-tuple-element.119) | copy-start | bytes 393220
  207.7 57.9 %all-to-all-start.1 = ((bf16[8,2,4096]{2,1,0:T(2,128)(2,1)}), bf16[8,2,4096]{2,1,0:T(2,128)(2,1)S(1)}, u32[]{:S(2)}, u32[]{:S(2)}) async-start(bf16[8,2,4096]{2,1,0:T(2,128)(2,1)} %reshape.393), calls=%async_computation.1 | async-start | bytes 262144 | tf_op jit(solution)/shard_map/all_to_all | solution.py:84
  260.2 11.9 %copy-start.18 = (bf16[1,128,512]{2,1,0:T(8,128)(2,1)S(1)}, bf16[1,128,512]{2,1,0:T(8,128)(2,1)}, u32[]{:S(2)}) copy-start(bf16[1,128,512]{2,1,0:T(8,128)(2,1)} %param.21) | copy-start | bytes 393220
  265.6 12.4 %all-to-all-start.3 = ((bf16[8,2,12288]{2,1,0:T(2,128)(2,1)}), bf16[8,2,12288]{2,1,0:T(2,128)(2,1)S(1)}, u32[]{:S(2)}, u32[]{:S(2)}) async-start(bf16[8,2,12288]{2,1,0:T(2,128)(2,1)} %reshape.395), calls=%async_computation.4 | async-start | bytes 786432 | tf_op jit(solution)/shard_map/all_to_all | solution.py:152
  271.3 277.5 %all-reduce.3.cloned.1.call-start = ((), (), s32[]{:S(2)}) async-start(), calls=%async_computation.7 | async-start | bytes 8388608 | tf_op jit(solution)/shard_map/psum | solution.py:160
  273.3 6.2 %copy-start.13 = (bf16[1,128,512]{2,1,0:T(8,128)(2,1)S(1)}, bf16[1,128,512]{2,1,0:T(8,128)(2,1)}, u32[]{:S(2)}) copy-start(bf16[1,128,512]{2,1,0:T(8,128)(2,1)} %param.15) | copy-start | bytes 393220
  273.3 6.2 %copy-start.27 = (f32[128]{0:T(128)S(1)}, f32[128]{0:T(128)}, u32[]{:S(2)}) copy-start(f32[128]{0:T(128)} %copy-done.26) | copy-start | bytes 1540
  281.8 1.0 copy-start.7
  (3 other events, 1.9 us)
Sparse Core Ops, SparseCore 0:
  24.2 43.1 all-gather.1
  202.7 53.9 reduce-scatter.1
  281.9 266.7 all-reduce.2
where the time goes:
time: 561 us; the launch traced here: 559 us
  waiting for transfers between devices  348 us (62%)
  local copies, waits for them, and re-layouts  90.9 us (16%)
  other arithmetic  41.3 us (7%)
  matrix products  35.3 us (6%)
  starting transfers between devices  16.3 us (3%)
  between operations  14 us (2%)
  blocking collectives  12.6 us (2%)
    psum x1, waiting for transfers between devices, body(): lax.psum((local_qkv, local_out), ('dp', 'seq', 'head'))  264 us
    reduce_scatter x1, waiting for transfers between devices, body(): lax.psum_scatter(pair_sums.reshape(seq_length, local_heads, 2 * HD), 'seq...  43 us
    all_gather x1, waiting for transfers between devices, body(): pair_all = lax.all_gather(pair_local, 'seq', axis=0, tiled=True)  36.5 us
    scatter-add x2, other arithmetic, scatter_step(): carried = carried.at[key_rows.reshape(-1)].add(both_parts)  20 us
    dot_general x4, matrix products, query_scores(): jnp.einsum('gqhe,gnkhe->ghqnk', query_blk, key_blk, preferred_element_typ...  15.7 us
    all_to_all x1, blocking collectives, body(): lax.all_to_all(packed, 'head', split_axis=1, concat_axis=0, tiled=True)  12.6 us
    reshape x4, local copies, waits for them, and re-layouts, query_scores(): return scores.reshape(scores.shape[0], scores.shape[1], scores.shape[2], -1)  12.5 us
  transfers between devices with their start and end apart: 6, of which 4 were waited for; matrix products, arithmetic and copies ran while one was open for 10% of the time, Pallas kernels for 0%

commit v1 on v0

--- a/solution.py
+++ b/solution.py
@@ -10,6 +10,11 @@
 BLK = 128
 NNZ = 9
 EPSILON = 1e-05
+
+
+def by_each_axis(array_2, first, second):
+    half = lax.psum(array_2, first)
+    return lax.psum(half, second)
 
 
 def normalize(token_rows):
@@ -157,7 +162,7 @@
     grad_input = ((grad_hidden - normed * inner) / spread).astype(jnp.bfloat16)
     local_qkv = jnp.einsum("td,tc->dc", hidden, grad_packed, preferred_element_type=jnp.float32)
     local_out = jnp.einsum("td,tc->dc", grad_rows, attended_tok, preferred_element_type=jnp.float32)
-    total_qkv, total_out = lax.psum((local_qkv, local_out), ("dp", "seq", "head"))
+    total_qkv, total_out = by_each_axis((local_qkv, local_out), ("seq", "head"), "dp")
     own_qkv = lax.dynamic_slice_in_dim(
         total_qkv, head_pos * local_heads * 3 * HD, local_heads * 3 * HD, 1
     )

time: 561 us -> 1010 us (1.80)
  waiting for transfers between devices: 348 us -> 798 us
    psum x1 -> x2, waiting for transfers between devices: 264 us -> 714 us  [the longest x1 618 us: by_each_axis(): half = lax.psum(array_2, first)]
  transfers between devices with their start and end apart: 6 -> 7, of which waited for: 4 -> 5; matrix products, arithmetic and copies ran while one was open for 10% -> 6% of each run, Pallas kernels for 0% -> 0%
where the time goes in v1:
time: 1010 us
  waiting for transfers between devices  798 us (79%)
  local copies, waits for them, and re-layouts  90 us (9%)
  other arithmetic  41.3 us (4%)
  matrix products  35.5 us (4%)
  starting transfers between devices  16.3 us (2%)
  between operations  14.1 us (1%)
  blocking collectives  12.6 us (1%)
    psum x1, waiting for transfers between devices, by_each_axis(): half = lax.psum(array_2, first)  618 us
    psum x1, waiting for transfers between devices, by_each_axis(): return lax.psum(half, second)  96.4 us
    reduce_scatter x1, waiting for transfers between devices, body(): lax.psum_scatter(pair_sums.reshape(seq_length, local_heads, 2 * HD), 'seq...  43.1 us
    all_gather x1, waiting for transfers between devices, body(): pair_all = lax.all_gather(pair_local, 'seq', axis=0, tiled=True)  36.5 us
  transfers between devices with their start and end apart: 7, of which 5 were waited for; matrix products, arithmetic and copies ran while one was open for 6% of the time, Pallas kernels for 0%

profile of v1, /device:TPU:2, one launch (start us, length us, event | category | flops | bytes accessed | tf_op | source)
XLA Modules:
  0.0 1008.5 jit_solution(12251053179627305069)
XLA Ops:
  10.6 12.6 %all_to_all.63 = bf16[128,8,192]{0,2,1:T(8,128)(2,1)S(1)} all-to-all(bf16[128,8,192]{0,2,1:T(8,128)(2,1)S(1)} %bitcast.271), channel_id=1, replica_groups=mesh['dp'=4,'seq'=8,'head'=8] {'head'}, dimensions={1} | all-to-all | bytes 786432 | tf_op jit(solution)/shard_map/all_to_all | solution.py:63
  25.1 4.8 all-to-all-start.2
  30.9 36.5 %all-gather.2.cloned.1.call-done = bf16[8192,1,128]{0,2,1:T(8,128)(2,1)} async-done(((bf16[1024,1,128]{0,2,1:T(8,128)(2,1)}), bf16[8192,1,128]{0,2,1:T(8,128)(2,1)}) %all-gather.2.cloned.1.call-update) | async-done | bytes 2097168 | tf_op jit(solution)/shard_map/all_gather | solution.py:66
  67.4 4.1 copy.119
  72.1 40.4 %while.24 = (s32[]{:T(128)}, bf16[2,4,128,1,64]{2,4,1,3,0:T(8,128)(2,1)}, f32[2,4,1,128]{3,1,2,0:T(4,128)}, s32[2,4,9]{2,1,0:T(4,128)S(1)}, bf16[64,128,1,128]{3...) while((s32[]{:T(128)}, ...), condition=%wide.region_4.7_spmd, body=%wide.region_1.6_spmd.sunk | while | flops 156931296 | bytes 39141280 | solution.py:84
  73.5 3.4 gather_fusion
  76.9 1.7 copy.151
  80.7 3.7 fusion.80
  86.2 3.1 copy.153
  89.3 2.3 fusion.81
  93.7 3.4 gather_fusion
  97.1 1.7 copy.151
  100.9 3.7 fusion.80
  106.4 3.1 copy.153
  109.5 2.3 fusion.81
  114.1 2.5 broadcast_in_dim.54
  116.6 86.2 %while.25 = (s32[]{:T(128)}, f32[64,128,1,128]{3,1,0,2:T(8,128)}, bf16[2,4,128,1,64]{2,4,1,3,0:T(8,128)(2,1)}, s32[2,4,9]{2,1,0:T(4,128)S(1)}, bf16[2,4,128,1,64...) while((s32[]{:T(128)}, f32[64,128,1,128]{3,1,0,2:T(8,128)}, ...), condition=%wide.region_8.11_spmd, body=%wide.region_6.10_spmd.sunk | while | flops 385783744 | bytes 64560684 | solution.py:149
  119.2 2.4 gather_fusion.3
  126.9 1.5 reshape.431
  128.4 2.5 copy.158
  130.9 2.1 reshape.432
  133.0 4.2 select_add_fusion.3
  137.2 3.1 copy.155
  140.3 2.5 fusion.94
  144.9 1.6 pad_maximum_fusion.3
  146.5 3.1 copy.157
  149.6 10.1 scatter_fusion
  162.3 2.4 gather_fusion.3
  171.4 2.5 copy.158
  173.9 2.1 reshape.432
  176.1 4.2 select_add_fusion.3
  180.3 3.1 copy.155
  183.4 2.5 fusion.94
  187.9 1.6 pad_maximum_fusion.3
  189.6 3.1 copy.157
  192.7 10.1 scatter_fusion
  204.7 2.3 reduce.9
  207.9 5.7 all-to-all-start.1
  213.9 43.1 %reduce-scatter.2.cloned.1.call-done = f32[1024,1,128]{2,1,0:T(1,128)} async-done(((f32[8192,1,128]{2,1,0:T(1,128)}), f32[1024,1,128]{2,1,0:T(1,128)}) %reduce-scatter.2.cloned.1.call-update) | async-done | bytes 524304 | tf_op jit(solution)/shard_map/reduce_scatter | solution.py:150
  258.4 2.0 pad_maximum_fusion.1
  260.4 4.1 reduce.10
  265.8 5.7 all-to-all-start.3
  273.6 4.6 all-to-all-done.3
  279.7 2.3 fusion.38
  282.1 617.6 %all-reduce.5.cloned.1.call-done = (f32[512,1536]{0,1:T(8,128)}, f32[512,512]{0,1:T(8,128)}) async-done(((f32[512,1536]{0,1:T(8,128)}, f32[512,512]{0,1:T(8,128)}), (f32[512,1536]{0,1:T(8,128)}, f32[512,512]{0,1:T(8,128)})) %all-reduce.5.cloned.1.call-update) | async-done | bytes 4194320 | tf_op jit(solution)/shard_map/psum | solution.py:16
  902.2 96.4 %all-reduce.7.cloned.1.call-done = (f32[512,1536]{0,1:T(8,128)}, f32[512,512]{0,1:T(8,128)}) async-done(((f32[512,1536]{0,1:T(8,128)}, f32[512,512]{0,1:T(8,128)}), (f32[512,1536]{0,1:T(8,128)}, f32[512,512]{0,1:T(8,128)})) %all-reduce.7.cloned.1.call-update) | async-done | bytes 4194320 | tf_op jit(solution)/shard_map/psum | solution.py:17
  998.7 1.8 constant_dynamic-slice_fusion.1
  1000.4 1.6 dynamic-slice_bitcast_fusion.4
  (203 shorter events, 53.1 us)
Async XLA Ops:
  7.2 1.8 copy-start
  7.2 60.2 %all-gather.2.cloned.1.call-start = ((), (), s32[]{:S(2)}) async-start(), calls=%async_computation.5 | async-start | bytes 2359296 | tf_op jit(solution)/shard_map/all_gather | solution.py:66
  9.0 15.1 %copy-start.6 = (bf16[512,512]{1,0:T(8,128)(2,1)S(1)}, bf16[512,512]{1,0:T(8,128)(2,1)}, u32[]{:S(2)}) copy-start(bf16[512,512]{1,0:T(8,128)(2,1)} %param.19) | copy-start | bytes 1572868
  9.0 15.1 %copy-start.17 = (bf16[1,128,512]{2,1,0:T(8,128)(2,1)S(1)}, bf16[1,128,512]{2,1,0:T(8,128)(2,1)}, u32[]{:S(2)}) copy-start(bf16[1,128,512]{2,1,0:T(8,128)(2,1)} %param.21) | copy-start | bytes 393220
  10.3 19.6 %copy-start.25 = (s32[1,64,9]{1,0,2:T(1,128)S(1)}, s32[1,64,9]{1,0,2:T(1,128)}, u32[]{:S(2)}) copy-start(s32[1,64,9]{1,0,2:T(1,128)} %param.17) | copy-start | bytes 6916
  10.4 19.8 %copy-start.28 = (f32[8]{0:T(128)S(1)}, f32[8]{0:T(128)}, u32[]{:S(2)}) copy-start(f32[8]{0:T(128)} %param.20) | copy-start | bytes 100
  10.4 20.4 %copy-start.3 = (s32[1,8192]{1,0:T(1,128)S(1)}, s32[1,8192]{1,0:T(1,128)}, u32[]{:S(2)}) copy-start(s32[1,8192]{1,0:T(1,128)} %param.16) | copy-start | bytes 98308
  25.1 87.4 %all-to-all-start.2 = ((bf16[128,8,64]{0,2,1:T(8,128)(2,1)}), bf16[128,8,64]{0,2,1:T(8,128)(2,1)S(1)}, u32[]{:S(2)}, u32[]{:S(2)}) async-start(bf16[128,8,64]{0,2,1:T(8,128)(2,1)} %bitcast.50), calls=%async_computation.2 | async-start | bytes 262144 | tf_op jit(solution)/shard_map/all_to_all | solution.py:95
  29.9 227.0 %reduce-scatter.2.cloned.1.call-start = ((), (), s32[]{:S(2)}) async-start(), calls=%async_computation.6 | async-start | bytes 4718592 | tf_op jit(solution)/shard_map/reduce_scatter | solution.py:150
  78.8 1.0 copy-start.4
  79.8 0.8 copy-start.19
  80.7 5.5 copy-start.22
  84.4 1.4 copy-start.2
  86.2 3.1 copy-start.23
  86.2 3.1 copy-start.10
  99.0 1.0 copy-start.4
  100.9 5.5 copy-start.22
  104.6 1.4 copy-start.2
  106.4 3.1 copy-start.23
  106.4 3.1 copy-start.10
  116.6 2.6 copy-start.20
  116.6 6.5 copy-start.8
  140.3 2.5 copy-start.1
  142.9 1.1 copy-start.5
  142.9 1.1 copy-start.14
  142.9 1.6 copy-start.9
  144.6 1.9 copy-start.15
  146.5 3.1 copy-start.24
  149.6 10.1 %copy-start.21 = (f32[2,4,1,128]{3,1,2,0:T(4,128)S(1)}, f32[2,4,1,128]{3,1,2,0:T(4,128)}, u32[]{:S(2)}) copy-start(f32[2,4,1,128]{3,1,2,0:T(4,128)} %copy-done.20) | copy-start | bytes 12292 | tf_op jit(solution)/shard_map/while
  159.7 2.5 copy-start.20
  159.7 6.4 copy-start.8
  183.4 2.5 copy-start.1
  185.9 1.1 copy-start.5
  186.0 1.1 copy-start.14
  186.0 1.6 copy-start.9
  187.6 1.9 copy-start.15
  189.6 3.1 copy-start.24
  192.7 10.1 copy-start.21
  202.7 0.9 copy-start.12
  203.7 9.9 copy-start.16
  207.9 57.9 %all-to-all-start.1 = ((bf16[8,2,4096]{2,1,0:T(2,128)(2,1)}), bf16[8,2,4096]{2,1,0:T(2,128)(2,1)S(1)}, u32[]{:S(2)}, u32[]{:S(2)}) async-start(bf16[8,2,4096]{2,1,0:T(2,128)(2,1)} %reshape.393), calls=%async_computation.1 | async-start | bytes 262144 | tf_op jit(solution)/shard_map/all_to_all | solution.py:89
  260.4 11.9 %copy-start.18 = (bf16[1,128,512]{2,1,0:T(8,128)(2,1)S(1)}, bf16[1,128,512]{2,1,0:T(8,128)(2,1)}, u32[]{:S(2)}) copy-start(bf16[1,128,512]{2,1,0:T(8,128)(2,1)} %param.21) | copy-start | bytes 393220
  265.8 12.4 %all-to-all-start.3 = ((bf16[8,2,12288]{2,1,0:T(2,128)(2,1)}), bf16[8,2,12288]{2,1,0:T(2,128)(2,1)S(1)}, u32[]{:S(2)}, u32[]{:S(2)}) async-start(bf16[8,2,12288]{2,1,0:T(2,128)(2,1)} %reshape.395), calls=%async_computation.4 | async-start | bytes 786432 | tf_op jit(solution)/shard_map/all_to_all | solution.py:157
  271.5 628.2 %all-reduce.5.cloned.1.call-start = ((), (), s32[]{:S(2)}) async-start(), calls=%async_computation.7 | async-start | bytes 8388608 | tf_op jit(solution)/shard_map/psum | solution.py:16
  273.6 6.1 copy-start.13
  273.6 6.1 copy-start.27
  282.1 617.7 %copy-start.7 = (bf16[512,512]{1,0:T(8,128)(2,1)S(1)}, bf16[512,512]{1,0:T(8,128)(2,1)}, u32[]{:S(2)}) copy-start(bf16[512,512]{1,0:T(8,128)(2,1)} %param.19) | copy-start | bytes 1572868
  282.1 716.6 %all-reduce.7.cloned.1.call-start = ((), (), s32[]{:S(2)}) async-start(), calls=%async_computation.8 | async-start | bytes 8388608 | tf_op jit(solution)/shard_map/psum | solution.py:17
  (4 other events, 2.7 us)
Sparse Core Ops, SparseCore 0:
  24.2 43.1 all-gather.1
  202.9 54.0 reduce-scatter.1
  282.2 617.5 all-reduce.4
  902.6 96.0 all-reduce.6
